TPU v7x, 32 devices: a whole 2x2x4 slice. The times are simulated.
32 devices in a mesh: row: 8 (over z, core), rep: 4 (over y, x).
Axes of the slice: x: 2, y: 2, z: 4, core: 2. Of those that a mesh axis runs over, the one named last changes fastest.
Arguments:
- features: bfloat16 [4096, 256], P(('row', 'rep')), may hold values from -6 to 6
- weight: bfloat16 [256, 256], replicated, may hold values from -0.375 to 0.375
- cotangent: bfloat16 [4096, 256], P(('row', 'rep')), may hold values from -6 to 6
- adjacency: bfloat16 [8, 4, 24, 128, 128], P('row', 'rep'), may hold values from -0.15625 to 0.15625
- tile_out: int32 [8, 4, 24], P('row', 'rep'), may hold values from 0 to 3
- tile_in: int32 [8, 4, 24], P('row', 'rep'), may hold values from 0 to 7
- live_count: int32 [8, 4], P('row', 'rep'), may hold values from 6 to 24, as said below
Outputs:
- activated: bfloat16 [4096, 256], P(('row', 'rep'))
- weight_grad: float32 [256, 256], replicated
- feature_grad: float32 [4096, 256], P(('row', 'rep'))
Inputs may be any that keep to these rules, and one draw needn't show every extreme that they name: `live_count`: live tile slots of one device; some device has all 24 slots live in every draw.
All inputs are finite; a program needn't handle non-finite values.
Results may differ from a plain program's by a relative error of at most 0.02.
Values may be sent and summed in bfloat16 or wider, within the bound.
A program may use at most 64 MiB of HBM per device.

v0:
```python
import math

import jax
import jax.numpy as jnp
from jax import lax
from jax.sharding import PartitionSpec as P


def tile_sums(adjacency, first_ids, second_ids, live_mask, table, count, transpose_tile):
    slot_count = adjacency.shape[0]
    block_rows = adjacency.shape[1]
    feat_width = table.shape[2]
    group_size = math.gcd(slot_count, 8)
    turns = slot_count // group_size
    items = (
        adjacency.reshape(turns, group_size, block_rows, block_rows),
        first_ids.reshape(turns, group_size),
        second_ids.reshape(turns, group_size),
        live_mask.reshape(turns, group_size),
    )

    def step_group(running, item):
        tile_group, read_ids, write_ids, live_group = item
        inputs = table[read_ids]
        if transpose_tile:
            products = jnp.einsum(
                "gji,gjf->gif", tile_group, inputs, preferred_element_type=jnp.float32
            )
        else:
            products = jnp.einsum(
                "gij,gjf->gif", tile_group, inputs, preferred_element_type=jnp.float32
            )
        onehot = (write_ids[None, :] == jnp.arange(count)[:, None]).astype(
            jnp.float32
        ) * live_group[None, :]
        running = running + jnp.einsum(
            "bg,gif->bif", onehot, products, precision=lax.Precision.HIGHEST
        )
        return (running, None)

    start = jnp.zeros((count, block_rows, feat_width), jnp.float32)
    running, unused = lax.scan(step_group, start, items)
    return running.reshape(count * block_rows, feat_width)


def add_sources(received):
    return jnp.sum(received.astype(jnp.float32), axis=0)


def body(features, weight, cotangent, adjacency, tile_out, tile_in, live_count):
    block_rows = features.shape[0]
    feat_width = features.shape[1]
    row_count = lax.axis_size("row")
    rep_count = lax.axis_size("rep")
    slot_count = adjacency.shape[2]
    adjacency = adjacency.reshape(slot_count, block_rows, block_rows)
    out_ids = tile_out.reshape(slot_count)
    in_ids = tile_in.reshape(slot_count)
    live_mask = (jnp.arange(slot_count) < live_count.reshape(())).astype(jnp.float32)
    gathered = lax.all_gather(features, "row", axis=0, tiled=True).reshape(
        row_count, block_rows, feat_width
    )
    partial_value = tile_sums(adjacency, in_ids, out_ids, live_mask, gathered, rep_count, False)
    aggregated = lax.psum_scatter(
        partial_value.astype(jnp.bfloat16), "rep", scatter_dimension=0, tiled=True
    )
    pre = jnp.dot(aggregated, weight, preferred_element_type=jnp.float32)
    sig = jax.nn.sigmoid(pre)
    activated = (pre * sig).astype(jnp.bfloat16)
    grad_pre = (cotangent.astype(jnp.float32) * sig * (1.0 + pre * (1.0 - sig))).astype(
        jnp.bfloat16
    )
    weight_part = jnp.dot(aggregated.T, grad_pre, preferred_element_type=jnp.float32)
    grad_rows = jnp.dot(grad_pre, weight.T, preferred_element_type=jnp.float32).astype(jnp.bfloat16)
    group_grads = lax.all_gather(grad_rows, "rep", axis=0, tiled=True)
    weight_grad = lax.psum(weight_part, ("row", "rep"))
    group_grads = group_grads.reshape(rep_count, block_rows, feat_width)
    returned = tile_sums(adjacency, out_ids, in_ids, live_mask, group_grads, row_count, True)
    rounded = returned.astype(jnp.bfloat16).reshape(row_count, block_rows, feat_width)
    feature_grad = add_sources(
        lax.all_to_all(rounded, "row", split_axis=0, concat_axis=0, tiled=True)
    )
    return (activated, weight_grad, feature_grad)


def solution(mesh):
    return jax.shard_map(
        body,
        mesh=mesh,
        in_specs=(
            P(("row", "rep"), None),
            P(),
            P(("row", "rep"), None),
            P("row", "rep", None, None, None),
            P("row", "rep", None),
            P("row", "rep", None),
            P("row", "rep"),
        ),
        out_specs=(P(("row", "rep"), None), P(), P(("row", "rep"), None)),
        check_vma=False,
    )
```

profile of v0, /device:TPU:0, one launch (start us, length us, event | category | flops | bytes accessed | tf_op | source)
XLA Modules:
  0.0 231.4 jit_solution(6620039171133740857)
XLA Ops:
  7.2 0.0 copy-start
  7.2 0.0 reduce-scatter.2.cloned.1.call-start
  7.9 0.0 copy-start.4
  7.9 0.5 broadcast.99
  8.4 0.1 copy-done.4
  8.6 0.0 copy-start.5
  8.6 0.7 reduce.6
  9.2 0.0 copy-done.5
  9.3 0.7 reduce.7
  9.9 0.1 reshape_reshape.14
  10.0 0.1 reshape_reshape.12
  10.1 16.7 %all_gather.6 = bf16[1024,256]{1,0:T(8,128)(2,1)S(1)} all-gather(bf16[128,256]{1,0:T(8,128)(2,1)} %param.11), channel_id=1, replica_groups=mesh['row'=8,'rep'=4] {'row'}, dimensions={0}, use_global_device_ids=true | all-gather | bytes 589824 | tf_op jit(solution)/shard_map/all_gather | solution.py:60
  26.8 10.8 %while.22 = (s32[]{:T(128)}, f32[4,128,256]{2,0,1:T(4,128)S(1)}, s32[3,8]{1,0:T(4,128)S(1)}, f32[3,8]{1,0:T(4,128)S(1)}, bf16[3,8,128,128]{3,2,1,0:T(8,128)(2,1)...) while((s32[]{:T(128)}, f32[4,128,256]{2,0,1:T(4,128)S(1)}, ...), condition=%wide.region_1.2_spmd.clone, body=%wide.region_0.1_spmd.clone.sunk | while | flops 79955032 | bytes 4985279 | solution.py:42
  26.8 0.6 gather_fusion
  27.4 1.2 fusion.61
  28.7 1.7 convolution_add_fusion.4
  30.5 0.6 gather_fusion
  31.0 1.2 fusion.61
  32.3 1.7 convolution_add_fusion.4
  34.1 0.6 gather_fusion
  34.7 1.2 fusion.61
  35.9 1.7 convolution_add_fusion.4
  37.6 0.0 copy-start.1
  37.6 0.8 copy.25
  38.4 0.0 reduce-scatter.2.cloned.1.call-update
  38.4 0.4 copy-done.1
  38.8 0.0 copy-start.3
  38.8 0.4 copy.13
  39.2 24.8 %reduce-scatter.2.cloned.1.call-done = bf16[128,256]{1,0:T(8,128)(2,1)} async-done(((bf16[512,256]{1,0:T(8,128)(2,1)}), bf16[128,256]{1,0:T(8,128)(2,1)}) %reduce-scatter.2.cloned.1.call-update) | async-done | bytes 65552 | tf_op jit(solution)/shard_map/reduce_scatter | solution.py:64
  64.0 0.0 copy-done
  64.0 0.0 copy-done.3
  64.0 1.7 multiply_convert_fusion
  65.7 0.2 convolution_convert_fusion
  65.9 9.3 %all_gather.7 = bf16[512,256]{1,0:T(8,128)(2,1)S(1)} all-gather(bf16[128,256]{1,0:T(8,128)(2,1)S(1)} %convolution_convert_fusion), channel_id=1, replica_groups=mesh['row'=8,'rep'=4] {'rep'}, dimensions={0}, use_global_device_ids=true | all-gather | bytes 327680 | tf_op jit(solution)/shard_map/all_gather | solution.py:75
  75.2 7.9 %while.23 = (s32[]{:T(128)}, f32[8,128,256]{2,0,1:T(8,128)S(1)}, s32[3,8]{1,0:T(4,128)S(1)}, f32[3,8]{1,0:T(4,128)S(1)}, bf16[3,8,128,128]{2,3,1,0:T(8,128)(2,1)...) while((s32[]{:T(128)}, f32[8,128,256]{2,0,1:T(8,128)S(1)}, ...), condition=%wide.region_5.6_spmd.clone, body=%wide.region_4.5_spmd.clone.sunk | while | flops 92800152 | bytes 6033855 | solution.py:42
  75.3 0.6 gather_fusion.1
  75.8 0.3 fusion.69
  76.1 1.7 convolution_add_fusion.5
  77.9 0.6 gather_fusion.1
  78.5 0.3 fusion.69
  78.8 1.7 convolution_add_fusion.5
  80.6 0.6 gather_fusion.1
  81.1 0.3 fusion.69
  81.4 1.7 convolution_add_fusion.5
  83.1 1.1 copy.24
  84.2 0.0 copy-start.2
  84.2 4.8 %all-to-all-start = ((bf16[8,128,256]{2,1,0:T(8,128)(2,1)}), bf16[8,128,256]{2,1,0:T(8,128)(2,1)S(1)}, u32[]{:S(2)}, u32[]{:S(2)}) async-start(bf16[8,128,256]{2,1,0:T(8,128)(2,1)} %copy.24), calls=%async_computation.1 | async-start | bytes 1048576 | tf_op jit(solution)/shard_map/all_to_all | solution.py:81
  89.0 0.0 all-reduce.2.cloned.1.call-start
  89.0 0.0 copy-done.2
  89.0 0.9 fusion.31
  89.9 0.0 all-reduce.2.cloned.1.call-update
  90.0 14.4 %all-to-all-done = bf16[8,128,256]{2,1,0:T(8,128)(2,1)S(1)} async-done(((bf16[8,128,256]{2,1,0:T(8,128)(2,1)}), bf16[8,128,256]{2,1,0:T(8,128)(2,1)S(1)}, u32[]{:S(2)}, u32[]{:S(2)}) %all-to-all-start) | async-done | bytes 524320 | tf_op jit(solution)/shard_map/all_to_all | solution.py:81
  104.3 0.7 convert_reduce_fusion
  105.1 117.8 %all-reduce.2.cloned.1.call-done = f32[256,256]{1,0:T(8,128)} async-done(((f32[256,256]{1,0:T(8,128)}), f32[256,256]{1,0:T(8,128)}) %all-reduce.2.cloned.1.call-update) | async-done | bytes 262160 | tf_op jit(solution)/shard_map/psum | solution.py:76
  222.9 1.7 copy.44
  (27 shorter events, 0.2 us)
Async XLA Ops:
  7.2 56.8 %copy-start = (bf16[256,256]{1,0:T(8,128)(2,1)S(1)}, bf16[256,256]{1,0:T(8,128)(2,1)}, u32[]{:S(2)}) copy-start(bf16[256,256]{1,0:T(8,128)(2,1)} %param.12) | copy-start | bytes 393220
  7.2 56.8 %reduce-scatter.2.cloned.1.call-start = ((), (), s32[]{:S(2)}) async-start(), calls=%async_computation.2 | async-start | bytes 327680 | tf_op jit(solution)/shard_map/reduce_scatter | solution.py:64
  7.9 0.7 copy-start.4
  8.6 0.7 copy-start.5
  37.6 1.2 copy-start.1
  38.8 25.2 %copy-start.3 = (bf16[128,256]{1,0:T(8,128)(2,1)S(1)}, bf16[128,256]{1,0:T(8,128)(2,1)}, u32[]{:S(2)}) copy-start(bf16[128,256]{1,0:T(8,128)(2,1)} %param.13) | copy-start | bytes 196612
  84.2 4.8 %copy-start.2 = (bf16[128,256]{1,0:T(8,128)(2,1)S(1)}, bf16[128,256]{1,0:T(8,128)(2,1)}, u32[]{:S(2)}) copy-start(bf16[128,256]{1,0:T(8,128)(2,1)} %reduce-scatter.2.cloned.1.call-done) | copy-start | bytes 196612
  84.2 20.1 %all-to-all-start = ((bf16[8,128,256]{2,1,0:T(8,128)(2,1)}), bf16[8,128,256]{2,1,0:T(8,128)(2,1)S(1)}, u32[]{:S(2)}, u32[]{:S(2)}) async-start(bf16[8,128,256]{2,1,0:T(8,128)(2,1)} %copy.24), calls=%async_computation.1 | async-start | bytes 1048576 | tf_op jit(solution)/shard_map/all_to_all | solution.py:81
  89.0 133.9 %all-reduce.2.cloned.1.call-start = ((), (), s32[]{:S(2)}) async-start(), calls=%async_computation.3 | async-start | bytes 524288 | tf_op jit(solution)/shard_map/psum | solution.py:76
Sparse Core Ops, SparseCore 0:
  38.5 25.4 reduce-scatter.1
  95.9 126.9 all-reduce.1
where the time goes:
time: 232 us; the launch traced here: 231 us
  waiting for transfers between devices  157 us (68%)
  blocking collectives  26 us (11%)
  matrix products  17.5 us (8%)
  between operations  14.8 us (6%)
  local copies, waits for them, and re-layouts  8.77 us (4%)
  starting transfers between devices  4.83 us (2%)
    psum x1, waiting for transfers between devices, body(): weight_grad = lax.psum(weight_part, ('row', 'rep'))  118 us
    reduce_scatter x1, waiting for transfers between devices, body(): lax.psum_scatter(partial_value.astype(jnp.bfloat16), 'rep', scatter_dimen...  24.8 us
    all_gather x1, blocking collectives, body(): lax.all_gather(features, 'row', axis=0, tiled=True)  16.7 us
    all_to_all x1, waiting for transfers between devices, body(): lax.all_to_all(rounded, 'row', split_axis=0, concat_axis=0, tiled=True)  14.4 us
    dot_general x6, matrix products, step_group(): jnp.einsum('bg,gif->bif', onehot, products, precision=lax.Precision.HIGHEST)  10.2 us
    all_gather x1, blocking collectives, body(): group_grads = lax.all_gather(grad_rows, 'rep', axis=0, tiled=True)  9.29 us
    all_to_all x1, starting transfers between devices, body(): lax.all_to_all(rounded, 'row', split_axis=0, concat_axis=0, tiled=True)  4.75 us
  transfers between devices with their start and end apart: 3, of which 3 were waited for; matrix products, arithmetic and copies ran while one was open for 1% of the time, Pallas kernels for 0%

commit v1 on v0

v1 whole, which is shorter than its diff:
```python
import functools

import jax
import jax.numpy as jnp
from jax import lax
from jax.experimental import pallas as pl
from jax.experimental.pallas import tpu as pltpu
from jax.sharding import PartitionSpec as P

MESH = pl.DeviceIdType.MESH
F32 = jnp.float32
BF16 = jnp.bfloat16


def each(first, last, step):
    if last - first <= 4:
        for index in range(first, last):
            step(index)
    else:
        lax.fori_loop(first, last, lambda index, unused: (step(index), unused)[1], 0)


def dot(left, right):
    return jnp.dot(left, right, preferred_element_type=F32)


def kernel(
    Z, C, S,
    feat_ref, weight_hbm, cot_hbm, adj_ref, tout_ref, tin_ref, live_ref,
    act_ref, wgrad_ref, fgrad_ref,
    tiles, cum, fwd_adj, bwd_adj, feat, weight_ref, cot_ref,
    acc, own_part, part_send, part_recv, grads,
    pair_send, pair_recv, ret_send, ret_recv,
    w_part, w_pair_send, w_pair_recv, w_half, w_rep_send, w_rep_recv, w_z, w_all,
    pos,
    local_sem, feat_send_sem, feat_fwd_sem, feat_recv_sem,
    part_send_sem, part_recv_sem, grad_send_sem, grad_recv_sem,
    pair_send_sem, pair_recv_sem, ret_send_sem, ret_recv_sem,
    w_pair_sem, w_rep_send_sem, w_rep_recv_sem, w_z_send_sem, w_z_recv_sem,
    w_gather_send_sem, w_gather_recv_sem, w_last_sem,
):
    r = lax.axis_index("row")
    c = lax.axis_index("rep")
    z = r // 2
    k = r % 2
    pr = 2 * z + 1 - k
    B = tiles.shape[1]
    F = feat.shape[2]

    def z_at(d):
        return (z + d) % Z

    def z_from(d):
        return (z + Z - d) % Z

    def c_at(e):
        return (c + e) % C

    def c_from(e):
        return (c + C - e) % C

    def remote(src, dst, send_sem, recv_sem, **where):
        return pltpu.make_async_remote_copy(
            src_ref=src, dst_ref=dst, send_sem=send_sem, recv_sem=recv_sem,
            device_id=where, device_id_type=MESH,
        )

    def to_partner(src, dst, send_sem, recv_sem):
        return remote(src, dst, send_sem, recv_sem, row=pr)

    own_copy = pltpu.make_async_copy(feat_ref, feat.at[r], local_sem.at[0])
    tile_copy = pltpu.make_async_copy(adj_ref.at[0, 0], tiles, local_sem.at[1])
    weight_copy = pltpu.make_async_copy(weight_hbm, weight_ref, local_sem.at[2])
    cot_copy = pltpu.make_async_copy(cot_hbm, cot_ref, local_sem.at[3])
    own_copy.start()
    tile_copy.start()
    weight_copy.start()
    cot_copy.start()

    barrier = pltpu.get_barrier_semaphore()

    def greet(**where):
        pl.semaphore_signal(barrier, inc=1, device_id=where, device_id_type=MESH)

    greet(row=pr)
    each(1, Z, lambda d: greet(row=2 * z_at(d) + k))
    each(1, C, lambda e: greet(rep=c_at(e)))
    pl.semaphore_wait(barrier, 1 + (Z - 1) + (C - 1))

    def feat_send(d):
        return remote(
            feat_ref, feat.at[r], feat_send_sem.at[d], feat_recv_sem.at[r],
            row=2 * z_at(d) + k,
        )

    def feat_forward(d):
        q = 2 * z_from(d) + k
        return to_partner(feat.at[q], feat.at[q], feat_fwd_sem.at[d], feat_recv_sem.at[q])

    def feat_wait(q):
        to_partner(feat.at[q], feat.at[q], feat_fwd_sem.at[0], feat_recv_sem.at[q]).wait_recv()

    feat_pair = to_partner(feat_ref, feat.at[r], feat_fwd_sem.at[0], feat_recv_sem.at[r])
    each(1, Z, lambda d: feat_send(d).start())
    feat_pair.start()

    live = live_ref[0, 0]
    for s in range(S):
        pos[s] = jnp.where(s < live, tin_ref[0, 0, s] * C + tout_ref[0, 0, s], -1)
    tile_copy.wait()
    cum[S] = jnp.zeros((B, B), F32)
    for s in range(S):
        prev = jnp.int32(S)
        for other in range(s):
            prev = jnp.where(pos[other] == pos[s], other, prev)
        term = tiles[s].astype(F32)
        cum[s] = term + cum[prev] if s else term

    def place(zz, unused):
        for kk in range(2):
            for b in range(C):
                spot = (2 * zz + kk) * C + b
                last = jnp.int32(S)
                for s in range(S):
                    last = jnp.where(pos[s] == spot, s, last)
                block = cum[last]
                fwd_adj[zz, b * B:(b + 1) * B, kk * B:(kk + 1) * B] = block.astype(BF16)
                bwd_adj[2 * zz + kk, :, b * B:(b + 1) * B] = block.T.astype(BF16)
        return unused

    lax.fori_loop(0, Z, place, 0)

    def pair_feats(zz):
        return feat[pl.ds(2 * zz, 2)].reshape(2 * B, F)

    own_copy.wait()
    feat_wait(pr)
    acc[...] = dot(fwd_adj[z], pair_feats(z))

    def take(d):
        feat_wait(2 * z_from(d) + k)
        feat_forward(d).start()

    take(1)

    def add_chip(d):
        take(d + 1)
        zz = z_from(d)
        feat_wait(2 * zz + 1 - k)
        acc[...] += dot(fwd_adj[zz], pair_feats(zz))

    each(1, Z - 1, add_chip)
    end = z_from(Z - 1)
    feat_wait(2 * end + 1 - k)

    def part_of(b):
        rows = pl.ds(pl.multiple_of(b * B, B), B)
        return acc[rows] + dot(fwd_adj[end, rows], pair_feats(end))

    def part_copy(e):
        return remote(
            part_send.at[e], part_recv.at[c], part_send_sem.at[e], part_recv_sem.at[c],
            rep=c_at(e),
        )

    def send_part(e):
        part_send[e] = part_of(c_at(e)).astype(BF16)
        part_copy(e).start()

    each(1, C, send_part)
    own_part[...] = part_of(c)

    def add_part(e):
        src = c_from(e)
        remote(
            part_send.at[e], part_recv.at[src], part_send_sem.at[e], part_recv_sem.at[src],
            rep=c_at(e),
        ).wait_recv()
        own_part[...] += part_recv[src].astype(F32)

    weight_copy.wait()
    cot_copy.wait()
    each(1, C, add_part)

    agg = own_part[...].astype(BF16)
    weight = weight_ref[...]
    pre = dot(agg, weight)
    sig = jax.nn.sigmoid(pre)
    grad_pre = (cot_ref[...].astype(F32) * sig * (1.0 + pre * (1.0 - sig))).astype(BF16)
    grads[c] = lax.dot_general(
        grad_pre, weight, (((1,), (1,)), ((), ())), preferred_element_type=F32
    ).astype(BF16)

    def grad_copy(e):
        return remote(
            grads.at[c], grads.at[c], grad_send_sem.at[e], grad_recv_sem.at[c], rep=c_at(e)
        )

    each(1, C, lambda e: grad_copy(e).start())
    act_ref[...] = (pre * sig).astype(BF16)

    w_part[...] = lax.dot_general(
        agg, grad_pre, (((0,), (0,)), ((), ())), preferred_element_type=F32
    ).reshape(w_part.shape)
    w_pair_send[...] = w_part[1 - k].astype(BF16)
    w_pair = to_partner(w_pair_send, w_pair_recv, w_pair_sem.at[0], w_pair_sem.at[1])
    w_pair.start()
    w_pair.wait_recv()
    w_half[...] = w_part[k] + w_pair_recv[...].astype(F32)
    w_rep_send[...] = w_half[...].astype(BF16)

    def w_rep_copy(e):
        dst = c_at(e)
        return remote(
            w_rep_send.at[dst], w_rep_recv.at[c], w_rep_send_sem.at[e], w_rep_recv_sem.at[c],
            rep=dst,
        )

    each(1, C, lambda e: w_rep_copy(e).start())

    def grad_wait(e):
        src = c_from(e)
        remote(
            grads.at[src], grads.at[src], grad_send_sem.at[e], grad_recv_sem.at[src], rep=c_at(e)
        ).wait_recv()

    each(1, C, grad_wait)

    def returned(q):
        return dot(bwd_adj[q], grads[...].reshape(C * B, F))

    def pair_copy(j):
        zz = z_at(j)
        return to_partner(
            pair_send.at[zz], pair_recv.at[zz], pair_send_sem.at[zz], pair_recv_sem.at[zz]
        )

    def send_pair(j):
        zz = z_at(j)
        pair_send[zz] = returned(2 * zz + 1 - k).astype(BF16)
        pair_copy(j).start()

    each(1, Z + 1, send_pair)

    def add_w_rep(e):
        src = c_from(e)
        remote(
            w_rep_send.at[src], w_rep_recv.at[src], w_rep_send_sem.at[e], w_rep_recv_sem.at[src],
            rep=src,
        ).wait_recv()
        w_half[c] += w_rep_recv[src].astype(F32)

    each(1, C, add_w_rep)
    w_z[z] = w_half[c].astype(BF16)

    def w_z_copy(d):
        return remote(
            w_z.at[z], w_z.at[z], w_z_send_sem.at[d], w_z_recv_sem.at[z], row=2 * z_at(d) + k
        )

    each(1, Z, lambda d: w_z_copy(d).start())

    def joined(j):
        zz = z_at(j)
        value = returned(2 * zz + k)
        pair_copy(j).wait_recv()
        return value + pair_recv[zz].astype(F32)

    def ret_copy(d):
        return remote(
            ret_send.at[d], ret_recv.at[z], ret_send_sem.at[d], ret_recv_sem.at[z],
            row=2 * z_at(d) + k,
        )

    def send_ret(d):
        ret_send[d] = joined(d).astype(BF16)
        ret_copy(d).start()

    each(1, Z, send_ret)
    fgrad_ref[...] = joined(Z)

    def w_z_wait(d):
        src = z_from(d)
        remote(
            w_z.at[src], w_z.at[src], w_z_send_sem.at[d], w_z_recv_sem.at[src],
            row=2 * src + k,
        ).wait_recv()

    each(1, Z, w_z_wait)
    w_all[k, c] = jnp.sum(w_z[...].astype(F32), axis=0).astype(BF16)

    def w_gather_copy(e):
        return remote(
            w_all.at[k, c], w_all.at[k, c], w_gather_send_sem.at[e], w_gather_recv_sem.at[c],
            rep=c_at(e),
        )

    each(1, C, lambda e: w_gather_copy(e).start())

    def w_gather_wait(e):
        src = c_from(e)
        remote(
            w_all.at[k, src], w_all.at[k, src], w_gather_send_sem.at[e],
            w_gather_recv_sem.at[src], rep=src,
        ).wait_recv()

    each(1, C, w_gather_wait)
    w_last = to_partner(w_all.at[k], w_all.at[k], w_last_sem.at[0], w_last_sem.at[1])
    w_last.start()
    to_partner(w_all.at[1 - k], w_all.at[1 - k], w_last_sem.at[0], w_last_sem.at[1]).wait_recv()
    wgrad_ref[...] = w_all[...].astype(F32).reshape(wgrad_ref.shape)

    def add_ret(d):
        src = z_from(d)
        remote(
            ret_send.at[d], ret_recv.at[src], ret_send_sem.at[d], ret_recv_sem.at[src],
            row=2 * src + k,
        ).wait_recv()
        fgrad_ref[...] += ret_recv[src].astype(F32)

    each(1, Z, add_ret)

    feat_pair.wait_send()
    w_pair.wait_send()
    w_last.wait_send()
    pair_copy(Z).wait_send()

    def drain_z(d):
        feat_send(d).wait_send()
        feat_forward(d).wait_send()
        pair_copy(d).wait_send()
        w_z_copy(d).wait_send()
        ret_copy(d).wait_send()

    def drain_c(e):
        part_copy(e).wait_send()
        grad_copy(e).wait_send()
        w_rep_copy(e).wait_send()
        w_gather_copy(e).wait_send()

    each(1, Z, drain_z)
    each(1, C, drain_c)


def solution(mesh):
    R = mesh.shape["row"]
    C = mesh.shape["rep"]
    Z = R // 2

    def body(features, weight, cotangent, adjacency, tile_out, tile_in, live_count):
        B, F = features.shape
        S = adjacency.shape[2]
        H = F // (2 * C)
        anywhere = pl.BlockSpec(memory_space=pl.ANY)
        scalar = pl.BlockSpec(memory_space=pltpu.SMEM)
        vector = pl.BlockSpec(memory_space=pltpu.VMEM)
        dma = pltpu.SemaphoreType.DMA
        return pl.pallas_call(
            functools.partial(kernel, Z, C, S),
            out_shape=(
                jax.ShapeDtypeStruct((B, F), BF16),
                jax.ShapeDtypeStruct(weight.shape, F32),
                jax.ShapeDtypeStruct((B, F), F32),
            ),
            in_specs=[anywhere] * 4 + [scalar] * 3,
            out_specs=(vector, vector, vector),
            scratch_shapes=[
                pltpu.VMEM((S, B, B), BF16),
                pltpu.VMEM((S + 1, B, B), F32),
                pltpu.VMEM((Z, C * B, 2 * B), BF16),
                pltpu.VMEM((R, B, C * B), BF16),
                pltpu.VMEM((R, B, F), BF16),
                pltpu.VMEM(weight.shape, BF16),
                pltpu.VMEM((B, F), BF16),
                pltpu.VMEM((C * B, F), F32),
                pltpu.VMEM((B, F), F32),
                pltpu.VMEM((C, B, F), BF16),
                pltpu.VMEM((C, B, F), BF16),
                pltpu.VMEM((C, B, F), BF16),
                pltpu.VMEM((Z, B, F), BF16),
                pltpu.VMEM((Z, B, F), BF16),
                pltpu.VMEM((Z, B, F), BF16),
                pltpu.VMEM((Z, B, F), BF16),
                pltpu.VMEM((2, C, H, F), F32),
                pltpu.VMEM((C, H, F), BF16),
                pltpu.VMEM((C, H, F), BF16),
                pltpu.VMEM((C, H, F), F32),
                pltpu.VMEM((C, H, F), BF16),
                pltpu.VMEM((C, H, F), BF16),
                pltpu.VMEM((Z, H, F), BF16),
                pltpu.VMEM((2, C, H, F), BF16),
                pltpu.SMEM((S,), jnp.int32),
                dma((4,)), dma((Z,)), dma((Z,)), dma((R,)),
                dma((C,)), dma((C,)), dma((C,)), dma((C,)),
                dma((Z,)), dma((Z,)), dma((Z,)), dma((Z,)),
                dma((2,)), dma((C,)), dma((C,)), dma((Z,)), dma((Z,)),
                dma((C,)), dma((C,)), dma((2,)),
            ],
            compiler_params=pltpu.CompilerParams(
                collective_id=0, has_side_effects=True, vmem_limit_bytes=60 * 2 ** 20
            ),
        )(features, weight, cotangent, adjacency, tile_out, tile_in, live_count)

    return jax.shard_map(
        body,
        mesh=mesh,
        in_specs=(
            P(("row", "rep"), None),
            P(),
            P(("row", "rep"), None),
            P("row", "rep", None, None, None),
            P("row", "rep", None),
            P("row", "rep", None),
            P("row", "rep"),
        ),
        out_specs=(P(("row", "rep"), None), P(), P(("row", "rep"), None)),
        check_vma=False,
    )
```

time: 232 us -> 41.1 us (0.18)
  waiting for transfers between devices: 157 us -> 0 us
  Pallas kernels: 0 us -> 35.7 us
  blocking collectives: 26 us -> 0 us
  matrix products: 17.5 us -> 0 us
  between operations: 14.8 us -> 1.29 us
  local copies, waits for them, and re-layouts: 8.77 us -> 3.84 us
  starting transfers between devices: 4.83 us -> 0 us
    psum x1 -> x0, waiting for transfers between devices: 118 us -> none  [body(): weight_grad = lax.psum(weight_part, ('row', 'rep'))]
    pallas_call x0 -> x1, Pallas kernels: none -> 35.7 us  [body(): pl.pallas_call(functools.partial(kernel, Z, C, S), out_shape=(jax.ShapeDt...]
    all_gather x2 -> x0, blocking collectives: 26 us -> none  [the longest x1 16.7 us: body(): lax.all_gather(features, 'row', axis=0, tiled=True)]
    reduce_scatter x1 -> x0, waiting for transfers between devices: 24.8 us -> none  [body(): lax.psum_scatter(partial_value.astype(jnp.bfloat16), 'rep', scatter_dimen...]
    dot_general x15 -> x0, matrix products: 17.5 us -> none  [the longest x6 10.2 us: step_group(): jnp.einsum('bg,gif->bif', onehot, products, precision=lax.Precision.HIGHEST)]
    all_to_all x1 -> x0, waiting for transfers between devices: 14.4 us -> none  [body(): lax.all_to_all(rounded, 'row', split_axis=0, concat_axis=0, tiled=True)]
    all_to_all x1 -> x0, starting transfers between devices: 4.75 us -> none  [body(): lax.all_to_all(rounded, 'row', split_axis=0, concat_axis=0, tiled=True)]
    gather x6 -> x0, local copies, waits for them, and re-layouts: 3.48 us -> none  [step_group(): inputs = table[read_ids]]
  transfers between devices with their start and end apart: 3 -> 0, of which waited for: 3 -> 0; matrix products, arithmetic and copies ran while one was open for 1% -> 0% of each run, Pallas kernels for 0% -> 0%
where the time goes in v1:
time: 41.1 us; the launch traced here: 40.9 us
  Pallas kernels  35.7 us (87%)
  local copies, waits for them, and re-layouts  3.84 us (9%)
  between operations  1.29 us (3%)
    pallas_call x1, Pallas kernels, body(): pl.pallas_call(functools.partial(kernel, Z, C, S), out_shape=(jax.ShapeDt...  35.7 us
    unnamed x5, local copies, waits for them, and re-layouts  3.84 us

profile of v1, /device:TPU:0, one launch (start us, length us, event | category | flops | bytes accessed | tf_op | source)
XLA Modules:
  0.0 40.9 jit_solution(5581373870804727489)
XLA Ops:
  1.3 35.7 %shard_map.94 = (bf16[128,256]{1,0:T(8,128)(2,1)}, f32[256,256]{1,0:T(8,128)}, f32[128,256]{1,0:T(8,128)}) custom-call(bf16[128,256]{1,0:T(8,128)(2,1)} %feat_ref.1, bf16[256,256]{1,0:T(8,128)(2,1)} %weight_hbm.1, bf16[128,256]{1,0:T(8,128)(2,1)} %cot_hbm.1, bf16[1,1,24,128,128]{4,3,2,1,0:T(8,128)(2,1)} %adj_ref.1, s32[1,1,24]{2,1,0:T(1,128)} %tout_ref.1, ...), custom_call_target="tpu_custom_call" | custom-call | tf_op jit(solution)/shard_map/pallas_call | solution.py:358
  37.0 1.5 %copy.14 = bf16[128,256]{1,0:T(8,128)(2,1)} copy(bf16[128,256]{1,0:T(8,128)(2,1)} %get-tuple-element.6) | data formatting | bytes 131072
  38.5 0.0 copy-start
  38.5 1.7 %copy.15 = f32[256,256]{1,0:T(8,128)} copy(f32[256,256]{1,0:T(8,128)} %get-tuple-element.7) | data formatting | bytes 524288
  40.2 0.0 copy-done
  40.2 0.7 %copy.16 = f32[128,256]{1,0:T(8,128)} copy(f32[128,256]{1,0:T(8,128)S(1)} %copy-done) | data formatting | bytes 262144
Async XLA Ops:
  38.5 1.7 %copy-start = (f32[128,256]{1,0:T(8,128)S(1)}, f32[128,256]{1,0:T(8,128)}, u32[]{:S(2)}) copy-start(f32[128,256]{1,0:T(8,128)} %get-tuple-element.8) | copy-start | bytes 393220

commit v2 on v1

v2 whole, which is shorter than its diff:
```python
import functools
import math

import jax
import jax.numpy as jnp
from jax import lax
from jax.experimental import pallas as pl
from jax.experimental.pallas import tpu as pltpu
from jax.sharding import PartitionSpec as P

MESH = pl.DeviceIdType.MESH
F32 = jnp.float32
BF16 = jnp.bfloat16


def each(first, last, step):
    if last - first <= 4:
        for index in range(first, last):
            step(index)
    else:
        lax.fori_loop(first, last, lambda index, unused: (step(index), unused)[1], 0)


def dot(left, right):
    return jnp.dot(left, right, preferred_element_type=F32)


def kernel(
    Z, C, S,
    feat_hbm, weight_hbm, cot_hbm, adj_hbm, tout_hbm, tin_hbm, live_ref,
    act_ref, wgrad_ref, fgrad_ref,
    tiles, cum, fwd_adj, bwd_adj, feat, weight_ref, cot_ref,
    acc, own_part, part_send, part_recv, grads,
    pair_send, pair_recv, ret_send, ret_recv,
    w_part, w_pair_send, w_pair_recv, w_half, w_rep_send, w_rep_recv, w_z, w_all,
    tout_ref, tin_ref, pos,
    local_sem, feat_send_sem, feat_fwd_sem, feat_recv_sem,
    part_send_sem, part_recv_sem, grad_send_sem, grad_recv_sem,
    pair_send_sem, pair_recv_sem, ret_send_sem, ret_recv_sem,
    w_pair_sem, w_rep_send_sem, w_rep_recv_sem, w_z_send_sem, w_z_recv_sem,
    w_gather_send_sem, w_gather_recv_sem, w_last_sem,
):
    r = lax.axis_index("row")
    c = lax.axis_index("rep")
    z = r // 2
    k = r % 2
    pr = 2 * z + 1 - k
    B = tiles.shape[1]
    W = feat.shape[3]
    halves = feat.shape[0]

    def cols(h):
        return slice(h * W, (h + 1) * W)

    def z_at(d):
        return (z + d) % Z

    def z_from(d):
        return (z + Z - d) % Z

    def c_at(e):
        return (c + e) % C

    def c_from(e):
        return (c + C - e) % C

    def remote(src, dst, send_sem, recv_sem, **where):
        return pltpu.make_async_remote_copy(
            src_ref=src, dst_ref=dst, send_sem=send_sem, recv_sem=recv_sem,
            device_id=where, device_id_type=MESH,
        )

    def to_partner(src, dst, send_sem, recv_sem):
        return remote(src, dst, send_sem, recv_sem, row=pr)

    barrier = pltpu.get_barrier_semaphore()

    def greet(**where):
        pl.semaphore_signal(barrier, inc=1, device_id=where, device_id_type=MESH)

    each(1, Z, lambda d: greet(row=2 * z_at(d) + k))
    each(1, C, lambda e: greet(rep=c_at(e)))
    greet(row=pr)

    own_copies = [
        pltpu.make_async_copy(feat_hbm.at[:, cols(h)], feat.at[h, r], local_sem.at[6 + h])
        for h in range(halves)
    ]
    tile_copy = pltpu.make_async_copy(adj_hbm.at[0, 0], tiles, local_sem.at[0])
    weight_copy = pltpu.make_async_copy(weight_hbm, weight_ref, local_sem.at[1])
    cot_copy = pltpu.make_async_copy(cot_hbm, cot_ref, local_sem.at[2])
    id_copies = [
        pltpu.make_async_copy(tout_hbm, tout_ref, local_sem.at[3]),
        pltpu.make_async_copy(tin_hbm, tin_ref, local_sem.at[4]),
    ]
    for copy in id_copies + [tile_copy] + own_copies + [weight_copy, cot_copy]:
        copy.start()
    pl.semaphore_wait(barrier, 1 + (Z - 1) + (C - 1))

    def feat_send(h, d):
        return remote(
            feat_hbm.at[:, cols(h)], feat.at[h, r], feat_send_sem.at[h, d],
            feat_recv_sem.at[h, r], row=2 * z_at(d) + k,
        )

    def feat_forward(h, d):
        q = 2 * z_from(d) + k
        return to_partner(
            feat.at[h, q], feat.at[h, q], feat_fwd_sem.at[h, d], feat_recv_sem.at[h, q]
        )

    def feat_wait(h, q):
        to_partner(
            feat.at[h, q], feat.at[h, q], feat_fwd_sem.at[h, 0], feat_recv_sem.at[h, q]
        ).wait_recv()

    feat_pairs = [
        to_partner(
            feat_hbm.at[:, cols(h)], feat.at[h, r], feat_fwd_sem.at[h, 0], feat_recv_sem.at[h, r]
        )
        for h in range(halves)
    ]
    for h in range(halves):
        each(1, Z, lambda d: feat_send(h, d).start())
        feat_pairs[h].start()

    for copy in id_copies:
        copy.wait()
    live = live_ref[0, 0]
    for s in range(S):
        pos[s] = jnp.where(s < live, tin_ref[0, 0, s] * C + tout_ref[0, 0, s], -1)
    tile_copy.wait()
    cum[S] = jnp.zeros((B, B), F32)
    for s in range(S):
        prev = jnp.int32(S)
        for other in range(s):
            prev = jnp.where(pos[other] == pos[s], other, prev)
        term = tiles[s].astype(F32)
        cum[s] = term + cum[prev] if s else term

    def place(zz, unused):
        for kk in range(2):
            for b in range(C):
                spot = (2 * zz + kk) * C + b
                last = jnp.int32(S)
                for s in range(S):
                    last = jnp.where(pos[s] == spot, s, last)
                block = cum[last]
                fwd_adj[zz, b * B:(b + 1) * B, kk * B:(kk + 1) * B] = block.astype(BF16)
                bwd_adj[2 * zz + kk, :, b * B:(b + 1) * B] = block.T.astype(BF16)
        return unused

    lax.fori_loop(0, Z, place, 0)

    def pair_feats(h, zz):
        return feat[h, pl.ds(2 * zz, 2)].reshape(2 * B, W)

    def part_copy(h, e):
        return remote(
            part_send.at[h, e], part_recv.at[h, c], part_send_sem.at[h, e],
            part_recv_sem.at[h, c], rep=c_at(e),
        )

    end = z_from(Z - 1)
    for h in range(halves):
        own_copies[h].wait()
        feat_wait(h, pr)
        acc[...] = dot(fwd_adj[z], pair_feats(h, z))

        def take(d):
            feat_wait(h, 2 * z_from(d) + k)
            feat_forward(h, d).start()

        def add_chip(d):
            take(d + 1)
            zz = z_from(d)
            feat_wait(h, 2 * zz + 1 - k)
            acc[...] += dot(fwd_adj[zz], pair_feats(h, zz))

        take(1)
        each(1, Z - 1, add_chip)
        feat_wait(h, 2 * end + 1 - k)

        def part_of(b):
            rows = pl.ds(pl.multiple_of(b * B, B), B)
            return acc[rows] + dot(fwd_adj[end, rows], pair_feats(h, end))

        def send_part(e):
            part_send[h, e] = part_of(c_at(e)).astype(BF16)
            part_copy(h, e).start()

        each(1, C, send_part)
        own_part[h] = part_of(c)

    weight_copy.wait()
    cot_copy.wait()
    weight = weight_ref[...]
    pre = None
    agg_halves = []
    for h in range(halves):

        def add_part(e):
            src = c_from(e)
            remote(
                part_send.at[h, e], part_recv.at[h, src], part_send_sem.at[h, e],
                part_recv_sem.at[h, src], rep=c_at(e),
            ).wait_recv()
            own_part[h] += part_recv[h, src].astype(F32)

        each(1, C, add_part)
        agg_half = own_part[h].astype(BF16)
        agg_halves.append(agg_half)
        term = dot(agg_half, weight[cols(h)])
        pre = term if pre is None else pre + term

    sig = jax.nn.sigmoid(pre)
    grad_pre = (cot_ref[...].astype(F32) * sig * (1.0 + pre * (1.0 - sig))).astype(BF16)

    def grad_copy(h, e):
        return remote(
            grads.at[h, c], grads.at[h, c], grad_send_sem.at[h, e], grad_recv_sem.at[h, c],
            rep=c_at(e),
        )

    def make_grads(h):
        grads[h, c] = lax.dot_general(
            grad_pre, weight[cols(h)], (((1,), (1,)), ((), ())), preferred_element_type=F32
        ).astype(BF16)

    def send_grads(h):
        each(1, C, lambda e: grad_copy(h, e).start())

    def grad_wait(h):
        def one(e):
            src = c_from(e)
            remote(
                grads.at[h, src], grads.at[h, src], grad_send_sem.at[h, e],
                grad_recv_sem.at[h, src], rep=c_at(e),
            ).wait_recv()

        each(1, C, one)

    make_grads(0)
    send_grads(0)

    agg = jnp.concatenate(agg_halves, axis=1)
    w_part[...] = lax.dot_general(
        agg, grad_pre, (((0,), (0,)), ((), ())), preferred_element_type=F32
    ).reshape(w_part.shape)
    w_pair_send[...] = w_part[1 - k].astype(BF16)
    w_pair = to_partner(w_pair_send, w_pair_recv, w_pair_sem.at[0], w_pair_sem.at[1])
    w_pair.start()
    for h in range(1, halves):
        make_grads(h)
    act_ref[...] = (pre * sig).astype(BF16)
    w_pair.wait_recv()
    w_half[...] = w_part[k] + w_pair_recv[...].astype(F32)
    w_rep_send[...] = w_half[...].astype(BF16)

    def w_rep_copy(e):
        dst = c_at(e)
        return remote(
            w_rep_send.at[dst], w_rep_recv.at[c], w_rep_send_sem.at[e], w_rep_recv_sem.at[c],
            rep=dst,
        )

    each(1, C, lambda e: w_rep_copy(e).start())
    for h in range(1, halves):
        send_grads(h)

    def returned(h, q):
        return dot(bwd_adj[q], grads[h].reshape(C * B, W))

    def pair_copy(h, j):
        zz = z_at(j)
        return to_partner(
            pair_send.at[h, zz], pair_recv.at[h, zz], pair_send_sem.at[h, zz],
            pair_recv_sem.at[h, zz],
        )

    def ret_copy(h, d):
        return remote(
            ret_send.at[h, d], ret_recv.at[h, z], ret_send_sem.at[h, d], ret_recv_sem.at[h, z],
            row=2 * z_at(d) + k,
        )

    def w_z_copy(d):
        return remote(
            w_z.at[z], w_z.at[z], w_z_send_sem.at[d], w_z_recv_sem.at[z], row=2 * z_at(d) + k
        )

    def return_half(h):
        def send_pair(j):
            zz = z_at(j)
            pair_send[h, zz] = returned(h, 2 * zz + 1 - k).astype(BF16)
            pair_copy(h, j).start()

        def joined(j):
            zz = z_at(j)
            value = returned(h, 2 * zz + k)
            pair_copy(h, j).wait_recv()
            return value + pair_recv[h, zz].astype(F32)

        def send_ret(d):
            ret_send[h, d] = joined(d).astype(BF16)
            ret_copy(h, d).start()

        grad_wait(h)
        each(1, Z + 1, send_pair)
        each(1, Z, send_ret)
        fgrad_ref[:, cols(h)] = joined(Z)

    def add_w_rep(e):
        src = c_from(e)
        remote(
            w_rep_send.at[src], w_rep_recv.at[src], w_rep_send_sem.at[e], w_rep_recv_sem.at[src],
            rep=src,
        ).wait_recv()
        w_half[c] += w_rep_recv[src].astype(F32)

    return_half(0)
    each(1, C, add_w_rep)
    w_z[z] = w_half[c].astype(BF16)
    each(1, Z, lambda d: w_z_copy(d).start())
    for h in range(1, halves):
        return_half(h)

    def w_z_wait(d):
        src = z_from(d)
        remote(
            w_z.at[src], w_z.at[src], w_z_send_sem.at[d], w_z_recv_sem.at[src],
            row=2 * src + k,
        ).wait_recv()

    each(1, Z, w_z_wait)
    w_all[k, c] = jnp.sum(w_z[...].astype(F32), axis=0).astype(BF16)

    def w_gather_copy(e):
        return remote(
            w_all.at[k, c], w_all.at[k, c], w_gather_send_sem.at[e], w_gather_recv_sem.at[c],
            rep=c_at(e),
        )

    each(1, C, lambda e: w_gather_copy(e).start())

    def add_ret(h, d):
        src = z_from(d)
        remote(
            ret_send.at[h, d], ret_recv.at[h, src], ret_send_sem.at[h, d],
            ret_recv_sem.at[h, src], row=2 * src + k,
        ).wait_recv()
        fgrad_ref[:, cols(h)] += ret_recv[h, src].astype(F32)

    for h in range(halves - 1):
        each(1, Z, lambda d: add_ret(h, d))

    def w_gather_wait(e):
        src = c_from(e)
        remote(
            w_all.at[k, src], w_all.at[k, src], w_gather_send_sem.at[e],
            w_gather_recv_sem.at[src], rep=src,
        ).wait_recv()

    each(1, C, w_gather_wait)
    w_last = to_partner(w_all.at[k], w_all.at[k], w_last_sem.at[0], w_last_sem.at[1])
    w_last.start()
    each(1, Z, lambda d: add_ret(halves - 1, d))
    to_partner(w_all.at[1 - k], w_all.at[1 - k], w_last_sem.at[0], w_last_sem.at[1]).wait_recv()
    wgrad_ref[...] = w_all[...].astype(F32).reshape(wgrad_ref.shape)

    w_pair.wait_send()
    w_last.wait_send()
    each(1, Z, lambda d: w_z_copy(d).wait_send())
    for h in range(halves):
        feat_pairs[h].wait_send()
        pair_copy(h, Z).wait_send()

        def drain_z(d):
            feat_send(h, d).wait_send()
            feat_forward(h, d).wait_send()
            pair_copy(h, d).wait_send()
            ret_copy(h, d).wait_send()

        def drain_c(e):
            part_copy(h, e).wait_send()
            grad_copy(h, e).wait_send()

        each(1, Z, drain_z)
        each(1, C, drain_c)

    def drain_w(e):
        w_rep_copy(e).wait_send()
        w_gather_copy(e).wait_send()

    each(1, C, drain_w)


def write_out(*refs):
    count = len(refs) // 2
    sem = refs[-1]
    copies = [
        pltpu.make_async_copy(refs[i], refs[count + i], sem.at[i]) for i in range(count)
    ]
    for copy in copies:
        copy.start()
    for copy in copies:
        copy.wait()


def solution(mesh):
    R = mesh.shape["row"]
    C = mesh.shape["rep"]
    Z = R // 2

    def body(features, weight, cotangent, adjacency, tile_out, tile_in, live_count):
        B, F = features.shape
        S = adjacency.shape[2]
        H = F // (2 * C)
        N = 2
        W = F // N
        anywhere = pl.BlockSpec(memory_space=pl.ANY)
        vector = pl.BlockSpec(memory_space=pltpu.VMEM)
        dma = pltpu.SemaphoreType.DMA
        out_shape = (
            jax.ShapeDtypeStruct((B, F), BF16),
            jax.ShapeDtypeStruct(weight.shape, F32),
            jax.ShapeDtypeStruct((B, F), F32),
        )
        buffers = [
            ((S, B, B), BF16), ((S + 1, B, B), F32),
            ((Z, C * B, 2 * B), BF16), ((R, B, C * B), BF16),
            ((N, R, B, W), BF16), (weight.shape, BF16), ((B, F), BF16),
            ((C * B, W), F32), ((N, B, W), F32),
            ((N, C, B, W), BF16), ((N, C, B, W), BF16), ((N, C, B, W), BF16),
            ((N, Z, B, W), BF16), ((N, Z, B, W), BF16),
            ((N, Z, B, W), BF16), ((N, Z, B, W), BF16),
            ((2, C, H, F), F32), ((C, H, F), BF16), ((C, H, F), BF16), ((C, H, F), F32),
            ((C, H, F), BF16), ((C, H, F), BF16), ((Z, H, F), BF16), ((2, C, H, F), BF16),
        ]
        held = sum(math.prod(shape) * (4 if kind == F32 else 2) for shape, kind in buffers)
        results = pl.pallas_call(
            functools.partial(kernel, Z, C, S),
            out_shape=out_shape,
            in_specs=[pl.BlockSpec(memory_space=pltpu.HBM)] * 6
            + [pl.BlockSpec(memory_space=pltpu.SMEM)],
            out_specs=(vector, vector, vector),
            scratch_shapes=[pltpu.VMEM(shape, kind) for shape, kind in buffers] + [
                pltpu.SMEM(tile_out.shape, jnp.int32),
                pltpu.SMEM(tile_in.shape, jnp.int32),
                pltpu.SMEM((S,), jnp.int32),
                dma((6 + N,)), dma((N, Z)), dma((N, Z)), dma((N, R)),
                dma((N, C)), dma((N, C)), dma((N, C)), dma((N, C)),
                dma((N, Z)), dma((N, Z)), dma((N, Z)), dma((N, Z)),
                dma((2,)), dma((C,)), dma((C,)), dma((Z,)), dma((Z,)),
                dma((C,)), dma((C,)), dma((2,)),
            ],
            compiler_params=pltpu.CompilerParams(
                collective_id=0, has_side_effects=True,
                vmem_limit_bytes=min(held + 8 * 2 ** 20, 60 * 2 ** 20),
            ),
        )(*(
            pltpu.with_memory_space_constraint(arg, pltpu.HBM)
            for arg in (features, weight, cotangent, adjacency, tile_out, tile_in)
        ), live_count)
        return pl.pallas_call(
            write_out,
            out_shape=out_shape,
            in_specs=[vector] * 3,
            out_specs=(anywhere,) * 3,
            scratch_shapes=[dma((3,))],
            compiler_params=pltpu.CompilerParams(vmem_limit_bytes=4 * 2 ** 20),
        )(*results)

    return jax.shard_map(
        body,
        mesh=mesh,
        in_specs=(
            P(("row", "rep"), None),
            P(),
            P(("row", "rep"), None),
            P("row", "rep", None, None, None),
            P("row", "rep", None),
            P("row", "rep", None),
            P("row", "rep"),
        ),
        out_specs=(P(("row", "rep"), None), P(), P(("row", "rep"), None)),
        check_vma=False,
    )
```

time: 41.1 us -> 38.3 us (0.932)
  local copies, waits for them, and re-layouts: 3.84 us -> 0 us
  Pallas kernels: 35.7 us -> 36.8 us
    unnamed x5 -> x0, local copies, waits for them, and re-layouts: 3.84 us -> none
    pallas_call x1 -> x2, Pallas kernels: 35.7 us -> 36.8 us  [the longest x1 36.1 us: body(): pl.pallas_call(functools.partial(kernel, Z, C, S), out_shape=out_shape, i...]
where the time goes in v2:
time: 38.3 us; the launch traced here: 38.1 us
  Pallas kernels  36.8 us (96%)
  between operations  1.29 us (3%)
    pallas_call x1, Pallas kernels, body(): pl.pallas_call(functools.partial(kernel, Z, C, S), out_shape=out_shape, i...  36.1 us
    pallas_call x1, Pallas kernels, body(): pl.pallas_call(write_out, out_shape=out_shape, in_specs=[vector] * 3, out...  0.79 us

profile of v2, /device:TPU:0, one launch (start us, length us, event | category | flops | bytes accessed | tf_op | source)
XLA Modules:
  0.0 38.1 jit_solution(12094530268583242377)
XLA Ops:
  1.3 36.1 %shard_map.94 = (bf16[128,256]{1,0:T(8,128)(2,1)S(1)}, f32[256,256]{1,0:T(8,128)S(1)}, f32[128,256]{1,0:T(8,128)S(1)}) custom-call(bf16[128,256]{1,0:T(8,128)(2,1)} %feat_hbm.1, bf16[256,256]{1,0:T(8,128)(2,1)} %weight_hbm.1, bf16[128,256]{1,0:T(8,128)(2,1)} %cot_hbm.1, bf16[1,1,24,128,128]{4,3,2,1,0:T(8,128)(2,1)} %adj_hbm.1, s32[1,1,24]{2,1,0:T(1,128)} %tout_hbm.1, ...), custom_call_target="tpu_custom_call" | custom-call | tf_op jit(solution)/shard_map/pallas_call | solution.py:441
  37.3 0.8 %shard_map.95 = (bf16[128,256]{1,0:T(8,128)(2,1)}, f32[256,256]{1,0:T(8,128)}, f32[128,256]{1,0:T(8,128)}) custom-call(bf16[128,256]{1,0:T(8,128)(2,1)S(1)} %get-tuple-element.6.refs_0_, f32[256,256]{1,0:T(8,128)S(1)} %get-tuple-element.7.refs_1_, f32[128,256]{1,0:T(8,128)S(1)} %get-tuple-element.8.refs_2_), custom_call_target="tpu_custom_call" | custom-call | tf_op jit(solution)/shard_map/pallas_call | solution.py:465

commit v3 on v2

--- a/solution.py
+++ b/solution.py
@@ -38,7 +38,7 @@
     part_send_sem, part_recv_sem, grad_send_sem, grad_recv_sem,
     pair_send_sem, pair_recv_sem, ret_send_sem, ret_recv_sem,
     w_pair_sem, w_rep_send_sem, w_rep_recv_sem, w_z_send_sem, w_z_recv_sem,
-    w_gather_send_sem, w_gather_recv_sem, w_last_sem,
+    w_gather_send_sem, w_gather_recv_sem,
 ):
     r = lax.axis_index("row")
     c = lax.axis_index("rep")
@@ -81,6 +81,7 @@
     each(1, Z, lambda d: greet(row=2 * z_at(d) + k))
     each(1, C, lambda e: greet(rep=c_at(e)))
     greet(row=pr)
+    each(1, C, lambda e: greet(row=pr, rep=c_at(e)))
 
     own_copies = [
         pltpu.make_async_copy(feat_hbm.at[:, cols(h)], feat.at[h, r], local_sem.at[6 + h])
@@ -95,7 +96,7 @@
     ]
     for copy in id_copies + [tile_copy] + own_copies + [weight_copy, cot_copy]:
         copy.start()
-    pl.semaphore_wait(barrier, 1 + (Z - 1) + (C - 1))
+    pl.semaphore_wait(barrier, 1 + (Z - 1) + 2 * (C - 1))
 
     def feat_send(h, d):
         return remote(
@@ -318,10 +319,10 @@
         ).wait_recv()
         w_half[c] += w_rep_recv[src].astype(F32)
 
-    return_half(0)
     each(1, C, add_w_rep)
     w_z[z] = w_half[c].astype(BF16)
     each(1, Z, lambda d: w_z_copy(d).start())
+    return_half(0)
     for h in range(1, halves):
         return_half(h)
 
@@ -335,13 +336,21 @@
     each(1, Z, w_z_wait)
     w_all[k, c] = jnp.sum(w_z[...].astype(F32), axis=0).astype(BF16)
 
-    def w_gather_copy(e):
-        return remote(
-            w_all.at[k, c], w_all.at[k, c], w_gather_send_sem.at[e], w_gather_recv_sem.at[c],
-            rep=c_at(e),
-        )
-
-    each(1, C, lambda e: w_gather_copy(e).start())
+    def w_gather_copy(kk, e):
+        return remote(
+            w_all.at[k, c], w_all.at[k, c], w_gather_send_sem.at[kk, e],
+            w_gather_recv_sem.at[k, c], row=2 * z + (k + kk) % 2, rep=c_at(e),
+        )
+
+    def w_gather_wait(kk, e):
+        src_k, src_c = (k + kk) % 2, c_from(e)
+        remote(
+            w_all.at[src_k, src_c], w_all.at[src_k, src_c], w_gather_send_sem.at[kk, e],
+            w_gather_recv_sem.at[src_k, src_c], row=2 * z + src_k, rep=src_c,
+        ).wait_recv()
+
+    for kk in range(2):
+        each(1 - kk, C, lambda e: w_gather_copy(kk, e).start())
 
     def add_ret(h, d):
         src = z_from(d)
@@ -351,25 +360,13 @@
         ).wait_recv()
         fgrad_ref[:, cols(h)] += ret_recv[h, src].astype(F32)
 
-    for h in range(halves - 1):
+    for h in range(halves):
         each(1, Z, lambda d: add_ret(h, d))
-
-    def w_gather_wait(e):
-        src = c_from(e)
-        remote(
-            w_all.at[k, src], w_all.at[k, src], w_gather_send_sem.at[e],
-            w_gather_recv_sem.at[src], rep=src,
-        ).wait_recv()
-
-    each(1, C, w_gather_wait)
-    w_last = to_partner(w_all.at[k], w_all.at[k], w_last_sem.at[0], w_last_sem.at[1])
-    w_last.start()
-    each(1, Z, lambda d: add_ret(halves - 1, d))
-    to_partner(w_all.at[1 - k], w_all.at[1 - k], w_last_sem.at[0], w_last_sem.at[1]).wait_recv()
+    for kk in range(2):
+        each(1 - kk, C, lambda e: w_gather_wait(kk, e))
     wgrad_ref[...] = w_all[...].astype(F32).reshape(wgrad_ref.shape)
 
     w_pair.wait_send()
-    w_last.wait_send()
     each(1, Z, lambda d: w_z_copy(d).wait_send())
     for h in range(halves):
         feat_pairs[h].wait_send()
@@ -388,11 +385,9 @@
         each(1, Z, drain_z)
         each(1, C, drain_c)
 
-    def drain_w(e):
-        w_rep_copy(e).wait_send()
-        w_gather_copy(e).wait_send()
-
-    each(1, C, drain_w)
+    each(1, C, lambda e: w_rep_copy(e).wait_send())
+    for kk in range(2):
+        each(1 - kk, C, lambda e: w_gather_copy(kk, e).wait_send())
 
 
 def write_out(*refs):
@@ -452,7 +447,7 @@
                 dma((N, C)), dma((N, C)), dma((N, C)), dma((N, C)),
                 dma((N, Z)), dma((N, Z)), dma((N, Z)), dma((N, Z)),
                 dma((2,)), dma((C,)), dma((C,)), dma((Z,)), dma((Z,)),
-                dma((C,)), dma((C,)), dma((2,)),
+                dma((2, C)), dma((2, C)),
             ],
             compiler_params=pltpu.CompilerParams(
                 collective_id=0, has_side_effects=True,

time: 38.3 us -> 36.4 us (0.950)
  Pallas kernels: 36.8 us -> 35 us
    pallas_call x1, Pallas kernels: 36.1 us -> 34.2 us  [body(): pl.pallas_call(functools.partial(kernel, Z, C, S), out_shape=out_shape, i...]
where the time goes in v3:
time: 36.4 us; the launch traced here: 36.3 us
  Pallas kernels  35 us (96%)
  between operations  1.29 us (4%)
    pallas_call x1, Pallas kernels, body(): pl.pallas_call(functools.partial(kernel, Z, C, S), out_shape=out_shape, i...  34.2 us
    pallas_call x1, Pallas kernels, body(): pl.pallas_call(write_out, out_shape=out_shape, in_specs=[vector] * 3, out...  0.79 us

profile of v3, /device:TPU:0, one launch (start us, length us, event | category | flops | bytes accessed | tf_op | source)
XLA Modules:
  0.0 36.3 jit_solution(15594041560738473587)
XLA Ops:
  1.3 34.2 %shard_map.94 = (bf16[128,256]{1,0:T(8,128)(2,1)S(1)}, f32[256,256]{1,0:T(8,128)S(1)}, f32[128,256]{1,0:T(8,128)S(1)}) custom-call(bf16[128,256]{1,0:T(8,128)(2,1)} %feat_hbm.1, bf16[256,256]{1,0:T(8,128)(2,1)} %weight_hbm.1, bf16[128,256]{1,0:T(8,128)(2,1)} %cot_hbm.1, bf16[1,1,24,128,128]{4,3,2,1,0:T(8,128)(2,1)} %adj_hbm.1, s32[1,1,24]{2,1,0:T(1,128)} %tout_hbm.1, ...), custom_call_target="tpu_custom_call" | custom-call | tf_op jit(solution)/shard_map/pallas_call | solution.py:436
  35.5 0.8 %shard_map.95 = (bf16[128,256]{1,0:T(8,128)(2,1)}, f32[256,256]{1,0:T(8,128)}, f32[128,256]{1,0:T(8,128)}) custom-call(bf16[128,256]{1,0:T(8,128)(2,1)S(1)} %get-tuple-element.6.refs_0_, f32[256,256]{1,0:T(8,128)S(1)} %get-tuple-element.7.refs_1_, f32[128,256]{1,0:T(8,128)S(1)} %get-tuple-element.8.refs_2_), custom_call_target="tpu_custom_call" | custom-call | tf_op jit(solution)/shard_map/pallas_call | solution.py:460
